TPU v7x, 32 devices: a whole 2x2x4 slice. The times are simulated.
32 devices in a mesh: inst: 2 (over x), panel: 8 (over z, y), obs: 2 (over core).
Axes of the slice: x: 2, y: 2, z: 4, core: 2. Of those that a mesh axis runs over, the one named last changes fastest.
Arguments:
- sources: bfloat16 [8, 4, 2048], P('inst', None, ('panel', 'obs')), may hold values from -12 to 12
- panel_positions: float32 [3, 2048], P(None, ('panel', 'obs')), may hold values from -1 to 1
- panel_copy: int32 [2048], P(('panel', 'obs')), may hold values from 0 to 2
- harmonic_numbers: int32 [3], replicated, may hold values from 1 to 3
- blade_count: int32 [1], replicated, may hold values from 3 to 34
- observer_ids: int32 [2, 128, 128], P('obs'), may hold values from 0 to 131071
- observer_radius: float32 [2, 128, 128], P('obs'), may hold values from 4 to 12
Outputs:
- pressure: float32 [2, 128, 2, 3, 128], P('obs', ('inst', 'panel'))
Inputs may be any that keep to these rules, and one draw needn't show every extreme that they name: `harmonic_numbers`: each is a harmonic number below 4. `panel_copy`: always below blade_count. `observer_ids`: an index on a grid of 256 polar by 512 azimuthal angles, not necessarily distinct.
All inputs are finite; a program needn't handle non-finite values.
Results may differ from a plain program's by a relative error of at most 0.0003.
Values may be sent and summed in bfloat16 or wider, within the bound.
No kernel may reach another device: no remote copies, remote signals or barrier semaphores. Data moves between devices by JAX's collectives and lax.ppermute only.
A program may use at most 64 MiB of HBM per device.

v0:
```python
import math

import jax
import jax.numpy as jnp
from jax import lax
from jax.sharding import PartitionSpec as P

NTHETA = 256
NPHI = 512


WAVE_UNIT = 0.05
QUADRUPLE_CIRCLE = 4.0 * 3.141592653589793
TWO_PI = 2.0 * 3.141592653589793


def dft_table(multiple_indices, per_chip_sample_sum, snapshot_number):
    sample_moments = jnp.arange(per_chip_sample_sum, dtype=jnp.int32)
    rotation_angles_list = multiple_indices[:, None] * sample_moments[None, :] % snapshot_number
    angles = TWO_PI * rotation_angles_list.astype(jnp.float32) / snapshot_number
    return jnp.concatenate([jnp.cos(angles), -jnp.sin(angles)], axis=0) / snapshot_number


def rotate_panels(spectra, panel_xyz, panel_copy, blade_count):
    angles = TWO_PI * panel_copy.astype(jnp.float32) / blade_count[0].astype(jnp.float32)
    cosine = jnp.cos(angles)
    sine_part = jnp.sin(angles)
    moved_xyz = jnp.stack(
        [
            cosine * panel_xyz[0] - sine_part * panel_xyz[1],
            sine_part * panel_xyz[0] + cosine * panel_xyz[1],
            panel_xyz[2],
        ]
    )
    along_x = spectra[:, :, 1]
    along_y = spectra[:, :, 2]
    moved = jnp.stack(
        [
            spectra[:, :, 0],
            cosine * along_x - sine_part * along_y,
            sine_part * along_x + cosine * along_y,
            spectra[:, :, 3],
        ],
        axis=2,
    )
    return (moved, moved_xyz)


def observer_coords(observer_ids, observer_radius):
    polar_index = observer_ids // NPHI
    azimuth_index = observer_ids % NPHI
    theta = 3.141592653589793 * (polar_index.astype(jnp.float32) + 0.5) / NTHETA
    azimuth = TWO_PI * azimuth_index.astype(jnp.float32) / NPHI
    sine_theta = jnp.sin(theta)
    return (
        observer_radius * sine_theta * jnp.cos(azimuth),
        observer_radius * sine_theta * jnp.sin(azimuth),
        observer_radius * jnp.cos(theta),
    )


def panel_term(coords, wavenumbers, spectrum, source_xyz):
    delta_x = coords[0] - source_xyz[0]
    delta_y = coords[1] - source_xyz[1]
    delta_z = coords[2] - source_xyz[2]
    distance = jnp.sqrt(delta_x * delta_x + delta_y * delta_y + delta_z * delta_z)
    inverse = 1.0 / distance
    spread = inverse / QUADRUPLE_CIRCLE
    near_field = spread * inverse * inverse
    real_parts = []
    imag_parts = []
    for number in range(wavenumbers.shape[0]):
        wavenumber = wavenumbers[number]
        phase_arg = wavenumber * distance
        cosine = jnp.cos(phase_arg)
        sine_part = jnp.sin(phase_arg)
        mono_real = spectrum[0, number, 0]
        mono_imag = spectrum[1, number, 0]
        dipole_real = (
            spectrum[0, number, 1] * delta_x
            + spectrum[0, number, 2] * delta_y
            + spectrum[0, number, 3] * delta_z
        )
        dipole_imag = (
            spectrum[1, number, 1] * delta_x
            + spectrum[1, number, 2] * delta_y
            + spectrum[1, number, 3] * delta_z
        )
        factor_real = cosine + phase_arg * sine_part
        factor_imag = phase_arg * cosine - sine_part
        real_parts.append(
            wavenumber * spread * (mono_real * sine_part - mono_imag * cosine)
            + near_field * (dipole_real * factor_real - dipole_imag * factor_imag)
        )
        imag_parts.append(
            wavenumber * spread * (mono_real * cosine + mono_imag * sine_part)
            + near_field * (dipole_real * factor_imag + dipole_imag * factor_real)
        )
    return (real_parts, imag_parts)


def accumulate(coords, wavenumbers, pressure_records, totals):
    harmonics = wavenumbers.shape[0]
    record_rows = pressure_records.shape[0]
    spec_rows = record_rows - 3
    components = spec_rows // (2 * harmonics)
    row_count = coords[0].shape[0]
    block_size = math.gcd(row_count, 2048)
    block_count = row_count // block_size
    surface_panel_total = pressure_records.shape[1]
    tile_size = min(256, surface_panel_total)
    tile_count = -(-surface_panel_total // tile_size)
    record_tiles = jnp.moveaxis(pressure_records.reshape(record_rows, tile_count, tile_size), 1, 0)
    block_coords = tuple((member.reshape(block_count, block_size, 1) for member in coords))

    def one_tile(current, record_tile):
        spectrum = record_tile[:spec_rows].reshape(2, harmonics, components, tile_size)
        source_xyz = record_tile[spec_rows:]

        def one_block(member):
            coords_part, sums_part = member
            real_parts, imag_parts = panel_term(coords_part, wavenumbers, spectrum, source_xyz)
            return tuple(
                (
                    running + jnp.sum(addend, axis=1)
                    for running, addend in zip(sums_part, real_parts + imag_parts)
                )
            )

        return (lax.map(one_block, (block_coords, current)), None)

    carried = tuple((member.reshape(block_count, block_size) for member in totals))
    finished, unused = lax.scan(one_tile, carried, record_tiles)
    return tuple((member.reshape(row_count) for member in finished))


def stack_rows(totals, harmonics):
    real_rows = jnp.stack(totals[:harmonics], axis=1)
    imag_rows = jnp.stack(totals[harmonics:], axis=1)
    return jnp.stack([real_rows, imag_rows], axis=1)


def per_device(
    sources,
    panel_positions,
    panel_copy,
    harmonic_numbers,
    blade_count,
    observer_ids,
    observer_radius,
):
    inst_count = lax.axis_size("inst")
    inst_here = lax.axis_index("inst")
    harmonics = harmonic_numbers.shape[0]
    components = sources.shape[1]
    per_chip_sample_sum = sources.shape[0]
    snapshot_number = per_chip_sample_sum * inst_count
    half_slab = sources.shape[2] // inst_count
    arrived = lax.all_to_all(sources, "inst", split_axis=2, concat_axis=0, tiled=True)
    dft_rows = dft_table(harmonic_numbers, snapshot_number, snapshot_number)
    spectra = jnp.einsum(
        "hn,ncp->hcp", dft_rows, arrived.astype(jnp.float32), precision=lax.Precision.HIGHEST
    )
    first_panel = inst_here * half_slab
    local_xyz = lax.dynamic_slice_in_dim(panel_positions, first_panel, half_slab, 1)
    local_copy = lax.dynamic_slice_in_dim(panel_copy, first_panel, half_slab, 0)
    spectra, local_xyz = rotate_panels(
        spectra.reshape(2, harmonics, components, half_slab), local_xyz, local_copy, blade_count
    )
    pressure_records = jnp.concatenate(
        [spectra.reshape(2 * harmonics * components, half_slab), local_xyz], axis=0
    )
    wavenumbers = (
        harmonic_numbers.astype(jnp.float32) * blade_count[0].astype(jnp.float32) * WAVE_UNIT
    )
    group_records = lax.all_gather(pressure_records, "obs", axis=1, tiled=True)
    coords = observer_coords(observer_ids[0], observer_radius[0])
    block_coords = tuple((member for member in coords))
    flat_coords = tuple((member.reshape(-1) for member in block_coords))
    empty_sums = tuple((jnp.zeros_like(flat_coords[0]) for number in range(2 * harmonics)))
    summed = accumulate(flat_coords, wavenumbers, group_records, empty_sums)
    shaped = tuple((member.reshape(block_coords[0].shape) for member in summed))
    own_spectra = lax.psum_scatter(
        stack_rows(shaped, harmonics), ("inst", "panel"), scatter_dimension=0, tiled=True
    )
    return own_spectra[None]


def solution(mesh):
    placed = (
        P("inst", None, ("panel", "obs")),
        P(None, ("panel", "obs")),
        P(("panel", "obs")),
        P(),
        P(),
        P("obs", None, None),
        P("obs", None, None),
    )
    return jax.shard_map(
        per_device,
        mesh=mesh,
        in_specs=placed,
        out_specs=P("obs", ("inst", "panel"), None, None, None),
        check_vma=False,
    )
```

profile of v0, /device:TPU:1, one launch (start us, length us, event | category | flops | bytes accessed | tf_op | source)
XLA Modules:
  0.0 345.0 jit_solution(16829351344804552264)
XLA Ops:
  25.5 186.8 %while.40 = (s32[]{:T(128)}, f32[8,2048]{1,0:T(8,128)S(1)}, f32[8,2048]{1,0:T(8,128)S(1)}, f32[8,2048]{1,0:T(8,128)S(1)}, f32[8,2048]{1,0:T(8,128)S(1)}, /*index...) while((s32[]{:T(128)}, f32[8,2048]{1,0:T(8,128)S(1)}, ...), condition=%wide.region_7.8_spmd, body=%wide.region_0.7_spmd.sunk | while | flops 37736448 | bytes 315133 | solution.py:130
  26.2 7.1 %fusion.85 = (f32[2048]{0:T(1024)S(1)}, f32[2048]{0:T(1024)S(1)}) fusion(f32[128]{0:T(128)S(1)} %get-tuple-element.539, f32[128]{0:T(128)S(1)} %get-tuple-element.540, f32[128]{0:T(128)S(1)} %get-tuple-element.541, f32[128]{0:T(128)S(1)} %get-tuple-element.542, f32[128]{0:T(128)S(1)} %get-tuple-element.543, f32[128]{0:T(128)S(1)} %get-tuple-element.544, ...), kind=kLoop, calls=%fused_computation.73.clone.1 | loop fusion | flops 12578816 | bytes 46600 | tf_op jit(solution)/shard_map/while/body/eval_jaxpr/while/body/eval_jaxpr/reduce_sum | solution.py:125
  33.4 7.1 %fusion.84 = (f32[2048]{0:T(1024)S(1)}, f32[2048]{0:T(1024)S(1)}) fusion(f32[128]{0:T(128)S(1)} %get-tuple-element.529, f32[128]{0:T(128)S(1)} %get-tuple-element.530, f32[128]{0:T(128)S(1)} %get-tuple-element.531, f32[128]{0:T(128)S(1)} %get-tuple-element.532, f32[128]{0:T(128)S(1)} %get-tuple-element.533, f32[128]{0:T(128)S(1)} %get-tuple-element.534, ...), kind=kLoop, calls=%fused_computation.75.clone.1 | loop fusion | flops 12578816 | bytes 46600 | tf_op jit(solution)/shard_map/while/body/eval_jaxpr/while/body/eval_jaxpr/reduce_sum | solution.py:125
  40.5 7.1 %fusion.83 = (f32[2048]{0:T(1024)S(1)}, f32[2048]{0:T(1024)S(1)}) fusion(f32[128]{0:T(128)S(1)} %get-tuple-element.514, f32[128]{0:T(128)S(1)} %get-tuple-element.515, f32[128]{0:T(128)S(1)} %get-tuple-element.516, f32[128]{0:T(128)S(1)} %get-tuple-element.517, f32[128]{0:T(128)S(1)} %get-tuple-element.518, f32[128]{0:T(128)S(1)} %get-tuple-element.519, ...), kind=kLoop, calls=%fused_computation.77.clone.1 | loop fusion | flops 12578816 | bytes 46600 | tf_op jit(solution)/shard_map/while/body/eval_jaxpr/while/body/eval_jaxpr/reduce_sum | solution.py:125
  49.6 7.1 %fusion.85 = (f32[2048]{0:T(1024)S(1)}, f32[2048]{0:T(1024)S(1)}) fusion(f32[128]{0:T(128)S(1)} %get-tuple-element.539, f32[128]{0:T(128)S(1)} %get-tuple-element.540, f32[128]{0:T(128)S(1)} %get-tuple-element.541, f32[128]{0:T(128)S(1)} %get-tuple-element.542, f32[128]{0:T(128)S(1)} %get-tuple-element.543, f32[128]{0:T(128)S(1)} %get-tuple-element.544, ...), kind=kLoop, calls=%fused_computation.73.clone.1 | loop fusion | flops 12578816 | bytes 46600 | tf_op jit(solution)/shard_map/while/body/eval_jaxpr/while/body/eval_jaxpr/reduce_sum | solution.py:125
  56.7 7.1 %fusion.84 = (f32[2048]{0:T(1024)S(1)}, f32[2048]{0:T(1024)S(1)}) fusion(f32[128]{0:T(128)S(1)} %get-tuple-element.529, f32[128]{0:T(128)S(1)} %get-tuple-element.530, f32[128]{0:T(128)S(1)} %get-tuple-element.531, f32[128]{0:T(128)S(1)} %get-tuple-element.532, f32[128]{0:T(128)S(1)} %get-tuple-element.533, f32[128]{0:T(128)S(1)} %get-tuple-element.534, ...), kind=kLoop, calls=%fused_computation.75.clone.1 | loop fusion | flops 12578816 | bytes 46600 | tf_op jit(solution)/shard_map/while/body/eval_jaxpr/while/body/eval_jaxpr/reduce_sum | solution.py:125
  63.8 7.1 %fusion.83 = (f32[2048]{0:T(1024)S(1)}, f32[2048]{0:T(1024)S(1)}) fusion(f32[128]{0:T(128)S(1)} %get-tuple-element.514, f32[128]{0:T(128)S(1)} %get-tuple-element.515, f32[128]{0:T(128)S(1)} %get-tuple-element.516, f32[128]{0:T(128)S(1)} %get-tuple-element.517, f32[128]{0:T(128)S(1)} %get-tuple-element.518, f32[128]{0:T(128)S(1)} %get-tuple-element.519, ...), kind=kLoop, calls=%fused_computation.77.clone.1 | loop fusion | flops 12578816 | bytes 46600 | tf_op jit(solution)/shard_map/while/body/eval_jaxpr/while/body/eval_jaxpr/reduce_sum | solution.py:125
  72.9 7.1 %fusion.85 = (f32[2048]{0:T(1024)S(1)}, f32[2048]{0:T(1024)S(1)}) fusion(f32[128]{0:T(128)S(1)} %get-tuple-element.539, f32[128]{0:T(128)S(1)} %get-tuple-element.540, f32[128]{0:T(128)S(1)} %get-tuple-element.541, f32[128]{0:T(128)S(1)} %get-tuple-element.542, f32[128]{0:T(128)S(1)} %get-tuple-element.543, f32[128]{0:T(128)S(1)} %get-tuple-element.544, ...), kind=kLoop, calls=%fused_computation.73.clone.1 | loop fusion | flops 12578816 | bytes 46600 | tf_op jit(solution)/shard_map/while/body/eval_jaxpr/while/body/eval_jaxpr/reduce_sum | solution.py:125
  80.1 7.1 %fusion.84 = (f32[2048]{0:T(1024)S(1)}, f32[2048]{0:T(1024)S(1)}) fusion(f32[128]{0:T(128)S(1)} %get-tuple-element.529, f32[128]{0:T(128)S(1)} %get-tuple-element.530, f32[128]{0:T(128)S(1)} %get-tuple-element.531, f32[128]{0:T(128)S(1)} %get-tuple-element.532, f32[128]{0:T(128)S(1)} %get-tuple-element.533, f32[128]{0:T(128)S(1)} %get-tuple-element.534, ...), kind=kLoop, calls=%fused_computation.75.clone.1 | loop fusion | flops 12578816 | bytes 46600 | tf_op jit(solution)/shard_map/while/body/eval_jaxpr/while/body/eval_jaxpr/reduce_sum | solution.py:125
  87.2 7.1 %fusion.83 = (f32[2048]{0:T(1024)S(1)}, f32[2048]{0:T(1024)S(1)}) fusion(f32[128]{0:T(128)S(1)} %get-tuple-element.514, f32[128]{0:T(128)S(1)} %get-tuple-element.515, f32[128]{0:T(128)S(1)} %get-tuple-element.516, f32[128]{0:T(128)S(1)} %get-tuple-element.517, f32[128]{0:T(128)S(1)} %get-tuple-element.518, f32[128]{0:T(128)S(1)} %get-tuple-element.519, ...), kind=kLoop, calls=%fused_computation.77.clone.1 | loop fusion | flops 12578816 | bytes 46600 | tf_op jit(solution)/shard_map/while/body/eval_jaxpr/while/body/eval_jaxpr/reduce_sum | solution.py:125
  96.3 7.1 %fusion.85 = (f32[2048]{0:T(1024)S(1)}, f32[2048]{0:T(1024)S(1)}) fusion(f32[128]{0:T(128)S(1)} %get-tuple-element.539, f32[128]{0:T(128)S(1)} %get-tuple-element.540, f32[128]{0:T(128)S(1)} %get-tuple-element.541, f32[128]{0:T(128)S(1)} %get-tuple-element.542, f32[128]{0:T(128)S(1)} %get-tuple-element.543, f32[128]{0:T(128)S(1)} %get-tuple-element.544, ...), kind=kLoop, calls=%fused_computation.73.clone.1 | loop fusion | flops 12578816 | bytes 46600 | tf_op jit(solution)/shard_map/while/body/eval_jaxpr/while/body/eval_jaxpr/reduce_sum | solution.py:125
  103.4 7.1 %fusion.84 = (f32[2048]{0:T(1024)S(1)}, f32[2048]{0:T(1024)S(1)}) fusion(f32[128]{0:T(128)S(1)} %get-tuple-element.529, f32[128]{0:T(128)S(1)} %get-tuple-element.530, f32[128]{0:T(128)S(1)} %get-tuple-element.531, f32[128]{0:T(128)S(1)} %get-tuple-element.532, f32[128]{0:T(128)S(1)} %get-tuple-element.533, f32[128]{0:T(128)S(1)} %get-tuple-element.534, ...), kind=kLoop, calls=%fused_computation.75.clone.1 | loop fusion | flops 12578816 | bytes 46600 | tf_op jit(solution)/shard_map/while/body/eval_jaxpr/while/body/eval_jaxpr/reduce_sum | solution.py:125
  110.5 7.1 %fusion.83 = (f32[2048]{0:T(1024)S(1)}, f32[2048]{0:T(1024)S(1)}) fusion(f32[128]{0:T(128)S(1)} %get-tuple-element.514, f32[128]{0:T(128)S(1)} %get-tuple-element.515, f32[128]{0:T(128)S(1)} %get-tuple-element.516, f32[128]{0:T(128)S(1)} %get-tuple-element.517, f32[128]{0:T(128)S(1)} %get-tuple-element.518, f32[128]{0:T(128)S(1)} %get-tuple-element.519, ...), kind=kLoop, calls=%fused_computation.77.clone.1 | loop fusion | flops 12578816 | bytes 46600 | tf_op jit(solution)/shard_map/while/body/eval_jaxpr/while/body/eval_jaxpr/reduce_sum | solution.py:125
  119.7 7.1 %fusion.85 = (f32[2048]{0:T(1024)S(1)}, f32[2048]{0:T(1024)S(1)}) fusion(f32[128]{0:T(128)S(1)} %get-tuple-element.539, f32[128]{0:T(128)S(1)} %get-tuple-element.540, f32[128]{0:T(128)S(1)} %get-tuple-element.541, f32[128]{0:T(128)S(1)} %get-tuple-element.542, f32[128]{0:T(128)S(1)} %get-tuple-element.543, f32[128]{0:T(128)S(1)} %get-tuple-element.544, ...), kind=kLoop, calls=%fused_computation.73.clone.1 | loop fusion | flops 12578816 | bytes 46600 | tf_op jit(solution)/shard_map/while/body/eval_jaxpr/while/body/eval_jaxpr/reduce_sum | solution.py:125
  126.8 7.1 %fusion.84 = (f32[2048]{0:T(1024)S(1)}, f32[2048]{0:T(1024)S(1)}) fusion(f32[128]{0:T(128)S(1)} %get-tuple-element.529, f32[128]{0:T(128)S(1)} %get-tuple-element.530, f32[128]{0:T(128)S(1)} %get-tuple-element.531, f32[128]{0:T(128)S(1)} %get-tuple-element.532, f32[128]{0:T(128)S(1)} %get-tuple-element.533, f32[128]{0:T(128)S(1)} %get-tuple-element.534, ...), kind=kLoop, calls=%fused_computation.75.clone.1 | loop fusion | flops 12578816 | bytes 46600 | tf_op jit(solution)/shard_map/while/body/eval_jaxpr/while/body/eval_jaxpr/reduce_sum | solution.py:125
  133.9 7.1 %fusion.83 = (f32[2048]{0:T(1024)S(1)}, f32[2048]{0:T(1024)S(1)}) fusion(f32[128]{0:T(128)S(1)} %get-tuple-element.514, f32[128]{0:T(128)S(1)} %get-tuple-element.515, f32[128]{0:T(128)S(1)} %get-tuple-element.516, f32[128]{0:T(128)S(1)} %get-tuple-element.517, f32[128]{0:T(128)S(1)} %get-tuple-element.518, f32[128]{0:T(128)S(1)} %get-tuple-element.519, ...), kind=kLoop, calls=%fused_computation.77.clone.1 | loop fusion | flops 12578816 | bytes 46600 | tf_op jit(solution)/shard_map/while/body/eval_jaxpr/while/body/eval_jaxpr/reduce_sum | solution.py:125
  143.0 7.1 %fusion.85 = (f32[2048]{0:T(1024)S(1)}, f32[2048]{0:T(1024)S(1)}) fusion(f32[128]{0:T(128)S(1)} %get-tuple-element.539, f32[128]{0:T(128)S(1)} %get-tuple-element.540, f32[128]{0:T(128)S(1)} %get-tuple-element.541, f32[128]{0:T(128)S(1)} %get-tuple-element.542, f32[128]{0:T(128)S(1)} %get-tuple-element.543, f32[128]{0:T(128)S(1)} %get-tuple-element.544, ...), kind=kLoop, calls=%fused_computation.73.clone.1 | loop fusion | flops 12578816 | bytes 46600 | tf_op jit(solution)/shard_map/while/body/eval_jaxpr/while/body/eval_jaxpr/reduce_sum | solution.py:125
  150.1 7.1 %fusion.84 = (f32[2048]{0:T(1024)S(1)}, f32[2048]{0:T(1024)S(1)}) fusion(f32[128]{0:T(128)S(1)} %get-tuple-element.529, f32[128]{0:T(128)S(1)} %get-tuple-element.530, f32[128]{0:T(128)S(1)} %get-tuple-element.531, f32[128]{0:T(128)S(1)} %get-tuple-element.532, f32[128]{0:T(128)S(1)} %get-tuple-element.533, f32[128]{0:T(128)S(1)} %get-tuple-element.534, ...), kind=kLoop, calls=%fused_computation.75.clone.1 | loop fusion | flops 12578816 | bytes 46600 | tf_op jit(solution)/shard_map/while/body/eval_jaxpr/while/body/eval_jaxpr/reduce_sum | solution.py:125
  157.3 7.1 %fusion.83 = (f32[2048]{0:T(1024)S(1)}, f32[2048]{0:T(1024)S(1)}) fusion(f32[128]{0:T(128)S(1)} %get-tuple-element.514, f32[128]{0:T(128)S(1)} %get-tuple-element.515, f32[128]{0:T(128)S(1)} %get-tuple-element.516, f32[128]{0:T(128)S(1)} %get-tuple-element.517, f32[128]{0:T(128)S(1)} %get-tuple-element.518, f32[128]{0:T(128)S(1)} %get-tuple-element.519, ...), kind=kLoop, calls=%fused_computation.77.clone.1 | loop fusion | flops 12578816 | bytes 46600 | tf_op jit(solution)/shard_map/while/body/eval_jaxpr/while/body/eval_jaxpr/reduce_sum | solution.py:125
  166.4 7.1 %fusion.85 = (f32[2048]{0:T(1024)S(1)}, f32[2048]{0:T(1024)S(1)}) fusion(f32[128]{0:T(128)S(1)} %get-tuple-element.539, f32[128]{0:T(128)S(1)} %get-tuple-element.540, f32[128]{0:T(128)S(1)} %get-tuple-element.541, f32[128]{0:T(128)S(1)} %get-tuple-element.542, f32[128]{0:T(128)S(1)} %get-tuple-element.543, f32[128]{0:T(128)S(1)} %get-tuple-element.544, ...), kind=kLoop, calls=%fused_computation.73.clone.1 | loop fusion | flops 12578816 | bytes 46600 | tf_op jit(solution)/shard_map/while/body/eval_jaxpr/while/body/eval_jaxpr/reduce_sum | solution.py:125
  173.5 7.1 %fusion.84 = (f32[2048]{0:T(1024)S(1)}, f32[2048]{0:T(1024)S(1)}) fusion(f32[128]{0:T(128)S(1)} %get-tuple-element.529, f32[128]{0:T(128)S(1)} %get-tuple-element.530, f32[128]{0:T(128)S(1)} %get-tuple-element.531, f32[128]{0:T(128)S(1)} %get-tuple-element.532, f32[128]{0:T(128)S(1)} %get-tuple-element.533, f32[128]{0:T(128)S(1)} %get-tuple-element.534, ...), kind=kLoop, calls=%fused_computation.75.clone.1 | loop fusion | flops 12578816 | bytes 46600 | tf_op jit(solution)/shard_map/while/body/eval_jaxpr/while/body/eval_jaxpr/reduce_sum | solution.py:125
  189.7 7.1 %fusion.85 = (f32[2048]{0:T(1024)S(1)}, f32[2048]{0:T(1024)S(1)}) fusion(f32[128]{0:T(128)S(1)} %get-tuple-element.539, f32[128]{0:T(128)S(1)} %get-tuple-element.540, f32[128]{0:T(128)S(1)} %get-tuple-element.541, f32[128]{0:T(128)S(1)} %get-tuple-element.542, f32[128]{0:T(128)S(1)} %get-tuple-element.543, f32[128]{0:T(128)S(1)} %get-tuple-element.544, ...), kind=kLoop, calls=%fused_computation.73.clone.1 | loop fusion | flops 12578816 | bytes 46600 | tf_op jit(solution)/shard_map/while/body/eval_jaxpr/while/body/eval_jaxpr/reduce_sum | solution.py:125
  196.8 7.1 %fusion.84 = (f32[2048]{0:T(1024)S(1)}, f32[2048]{0:T(1024)S(1)}) fusion(f32[128]{0:T(128)S(1)} %get-tuple-element.529, f32[128]{0:T(128)S(1)} %get-tuple-element.530, f32[128]{0:T(128)S(1)} %get-tuple-element.531, f32[128]{0:T(128)S(1)} %get-tuple-element.532, f32[128]{0:T(128)S(1)} %get-tuple-element.533, f32[128]{0:T(128)S(1)} %get-tuple-element.534, ...), kind=kLoop, calls=%fused_computation.75.clone.1 | loop fusion | flops 12578816 | bytes 46600 | tf_op jit(solution)/shard_map/while/body/eval_jaxpr/while/body/eval_jaxpr/reduce_sum | solution.py:125
  213.3 123.5 %reduce-scatter.2.cloned.1.call-done = f32[8,2,3,128]{3,0,2,1:T(8,128)} async-done(((f32[128,2,3,128]{3,0,2,1:T(8,128)}), f32[8,2,3,128]{3,0,2,1:T(8,128)}) %reduce-scatter.2.cloned.1.call-update) | async-done | bytes 24592 | tf_op jit(solution)/shard_map/reduce_scatter | solution.py:183
  (153 shorter events, 48.1 us)
Async XLA Ops:
  6.5 7.3 %copy-start = (f32[3,128]{1,0:T(4,128)S(1)}, f32[3,128]{1,0:T(4,128)}, u32[]{:S(2)}) copy-start(f32[3,128]{1,0:T(4,128)} %param.10) | copy-start | bytes 4612
  7.4 7.1 %copy-start.1 = (f32[1,128,128]{2,1,0:T(8,128)S(1)}, f32[1,128,128]{2,1,0:T(8,128)}, u32[]{:S(2)}) copy-start(f32[1,128,128]{2,1,0:T(8,128)} %param.15) | copy-start | bytes 196612
  7.4 7.1 %copy-start.2 = (s32[1,128,128]{2,1,0:T(8,128)S(1)}, s32[1,128,128]{2,1,0:T(8,128)}, u32[]{:S(2)}) copy-start(s32[1,128,128]{2,1,0:T(8,128)} %param.14) | copy-start | bytes 196612
  8.2 14.1 %all-to-all-start = ((bf16[2,2,512]{2,1,0:T(2,128)(2,1)}), bf16[2,2,512]{2,1,0:T(2,128)(2,1)S(1)}, u32[]{:S(2)}, u32[]{:S(2)}) async-start(bf16[2,2,512]{2,1,0:T(2,128)(2,1)} %reshape.275), calls=%async_computation | async-start | bytes 8192 | tf_op jit(solution)/shard_map/all_to_all | solution.py:159
  11.5 325.3 %reduce-scatter.2.cloned.1.call-start = ((), (), s32[]{:S(2)}) async-start(), calls=%async_computation.2 | async-start | bytes 417792 | tf_op jit(solution)/shard_map/reduce_scatter | solution.py:183
  12.2 0.7 copy-start.3
  13.0 0.7 copy-start.4
Sparse Core Ops, SparseCore 0:
  213.5 123.2 reduce-scatter.1
where the time goes:
time: 348 us; the launch traced here: 345 us
  other arithmetic  178 us (51%)
  waiting for transfers between devices  123 us (35%)
  local copies, waits for them, and re-layouts  21.1 us (6%)
  between operations  16.2 us (5%)
    reduce_sum x24, other arithmetic, one_block(): jnp.sum(addend, axis=1)  171 us
    reduce_scatter x1, waiting for transfers between devices, per_device(): lax.psum_scatter(stack_rows(shaped, harmonics), ('inst', 'panel'), scatte...  123 us
    dynamic_update_slice x48, local copies, waits for them, and re-layouts, one_tile(): return (lax.map(one_block, (block_coords, current)), None)  9.75 us
  transfers between devices with their start and end apart: 2, of which 1 were waited for; matrix products, arithmetic and copies ran while one was open for 2% of the time, Pallas kernels for 0%

commit v1 on v0

v1 whole, which is shorter than its diff:
```python
import functools
import math

import jax
import jax.numpy as jnp
import numpy as np
from jax import lax
from jax.experimental import pallas as pl
from jax.experimental.pallas import tpu as pltpu
from jax.sharding import PartitionSpec as P

NTHETA = 256
NPHI = 512
WAVE_UNIT = 0.05
TWO_PI = 2.0 * 3.141592653589793
LANES = 128
TILE = 256
CHUNK = 256
HELD_TILES = 8
FEATURES = 8
PARTS = 6
DEPTH = FEATURES * PARTS

HALF_SINE = (6.28317247, -10.33464405, 5.08745911, -1.11966943)


def split_parts(value):
    high = value.astype(jnp.bfloat16).astype(jnp.float32)
    rest = value - high
    middle = rest.astype(jnp.bfloat16).astype(jnp.float32)
    return high, middle, rest - middle


def pack_kernel(blades_ref, src_ref, pos_ref, copy_ref, out_ref):
    inst_here = lax.axis_index("inst")
    angle = TWO_PI * copy_ref[...].astype(jnp.float32) / blades_ref[0].astype(jnp.float32)
    cosine, sine = jnp.cos(angle), jnp.sin(angle)
    x, y, z = pos_ref[0:1, :], pos_ref[1:2, :], pos_ref[2:3, :]
    values = (cosine * x - sine * y, sine * x + cosine * y, z, cosine, sine)
    parts = [split_parts(value) for value in values]
    rows = [parts[i][j] for j in range(3) for i in range(5)]
    rows.append(jnp.zeros_like(z))
    own = jnp.where(inst_here == 0, jnp.concatenate(rows[:8], axis=0), jnp.concatenate(rows[8:], axis=0))
    terms = [src_ref[n].astype(jnp.float32) for n in range(src_ref.shape[0])]
    block = jnp.concatenate(terms + [own], axis=0).astype(jnp.bfloat16)

    def put(d, carry):
        out_ref[d] = block
        return carry

    lax.fori_loop(0, out_ref.shape[0], put, 0)


def pair_factors(t2, t0, orders):
    w = lax.rsqrt(t2)
    w3 = w * (1.0 / t2)
    t = t2 * w
    f = t - t0
    z = f * f
    s = jnp.float32(HALF_SINE[-1])
    for c in HALF_SINE[-2::-1]:
        s = s * z + jnp.float32(c)
    s = s * f
    q = s * s
    twice = 2.0 - q
    d = 4.0 - q
    cosine = w3 * twice
    sine = w3 * (s * (d * lax.rsqrt(d)))
    factors = {1: (cosine, sine)}
    if orders[-1] > 1:
        factors[2] = (twice * cosine - (w3 + w3), twice * sine)
    for m in range(3, orders[-1] + 1):
        (c1, s1), (c0, s0) = factors[m - 1], factors[m - 2]
        factors[m] = (twice * c1 - c0, twice * s1 - s0)
    return t, factors


def main_kernel(
    harm_ref, blades_ref, table_ref, got_ref, ids_ref, radius_ref, out_ref,
    feat_ref, hub_ref, coef_ref, acc_ref, rows_ref, *, insts, per_inst, comps, orders,
):
    block_rows = out_ref.shape[2]
    observers = block_rows * LANES
    groups = got_ref.shape[0] // insts
    tiles = groups * LANES // TILE
    held = min(HELD_TILES, tiles)
    per_tile = TILE // LANES
    src_rows = per_inst * comps
    count = len(orders)
    first = (lax.axis_index("inst") * lax.axis_size("panel") + lax.axis_index("panel")) * block_rows
    first = pl.multiple_of(first, 8)

    kappa = blades_ref[0].astype(jnp.float32) * WAVE_UNIT
    scale = kappa / TWO_PI

    ids = ids_ref[0, pl.ds(first, block_rows), :]
    radius = radius_ref[0, pl.ds(first, block_rows), :]
    theta = 3.141592653589793 * ((ids // NPHI).astype(jnp.float32) + 0.5) / NTHETA
    phi = TWO_PI * (ids % NPHI).astype(jnp.float32) / NPHI
    sine_theta = jnp.sin(theta)
    x1 = radius * sine_theta * jnp.cos(phi)
    x2 = radius * sine_theta * jnp.sin(phi)
    x3 = radius * jnp.cos(theta)
    hub = scale * radius
    features = (x1, x2, x3, jnp.ones_like(x1), radius * radius)
    for b in range(0, block_rows, 8):
        for i in range(FEATURES):
            value = features[i][b : b + 8] if i < len(features) else jnp.zeros((8, LANES), jnp.float32)
            rows_ref[i * 8 : (i + 1) * 8, :] = value
        for r in range(8):
            b1, b2, b3 = split_parts(rows_ref[pl.ds(r, FEATURES, stride=8), :])
            stack = [b1, b2, b3, b1, b2, b1, jnp.broadcast_to(hub[b + r : b + r + 1], (8, LANES))]
            stack.append(jnp.zeros((LANES - 8 * len(stack), LANES), jnp.float32))
            turned = jnp.concatenate(stack, axis=0).T
            at = slice((b + r) * LANES, (b + r + 1) * LANES)
            feat_ref[at, :] = turned[:, 0:DEPTH].astype(jnp.bfloat16)
            hub_ref[at, :] = jnp.broadcast_to(turned[:, DEPTH : DEPTH + 1], (LANES, LANES))

    row = lax.broadcasted_iota(jnp.int32, (8, TILE), 0)
    order_of_row = (row // 2 + 1).astype(jnp.float32)
    s2 = scale * scale
    s3 = s2 * scale
    far = s3 / (8.0 * 3.141592653589793)
    near = order_of_row * (s3 * 0.25)
    mono = order_of_row * (s2 * 0.25)

    def coefficients(first_tile):
        def one(j, carry):
            at = (first_tile + j) * per_tile
            src = [
                jnp.concatenate([got_ref[i * groups + at + p, 0:src_rows, :] for p in range(per_tile)], axis=1)
                for i in range(insts)
            ]
            src = jnp.concatenate(src, axis=0)
            spec = None
            for part in range(3):
                term = jnp.dot(table_ref[part], src, preferred_element_type=jnp.float32)
                spec = term if spec is None else spec + term
            turned_q, f1, f2, f3 = (spec[8 * c : 8 * c + 8] for c in range(4))
            geo = [
                jnp.concatenate(
                    [got_ref[i * groups + at + p, src_rows : src_rows + 8, :].astype(jnp.float32) for p in range(per_tile)],
                    axis=1,
                )
                for i in range(2)
            ]
            geo = [geo[i][r : r + 1] for i in range(2) for r in range(8)]
            y1, y2, y3, cosine, sine = (geo[i] + geo[5 + i] + geo[10 + i] for i in range(5))
            g1 = cosine * f1 - sine * f2
            g2 = sine * f1 + cosine * f2
            dipole = (g1, g2, f3, -(g1 * y1 + g2 * y2 + f3 * y3))
            square = y1 * y1 + y2 * y2 + y3 * y3
            distance = (-2.0 * s2 * y1, -2.0 * s2 * y2, -2.0 * s2 * y3, s2 * square, jnp.full_like(y1, s2))
            lifted = mono * turned_q
            zero = jnp.zeros((8, TILE), jnp.float32)

            def write(o, value):
                a1, a2, a3 = split_parts(value)
                coef_ref[o, j, 0:16, :] = jnp.concatenate([a1, a1], axis=0).astype(jnp.bfloat16)
                coef_ref[o, j, 16:32, :] = jnp.concatenate([a1, a2], axis=0).astype(jnp.bfloat16)
                coef_ref[o, j, 32:48, :] = jnp.concatenate([a2, a3], axis=0).astype(jnp.bfloat16)

            def keep(i, value):
                for p in range(per_tile):
                    rows_ref[(p * FEATURES + i) * 8 : (p * FEATURES + i + 1) * 8, :] = value[:, p * LANES : (p + 1) * LANES]

            def gathered(r):
                return jnp.concatenate(
                    [rows_ref[pl.ds(p * FEATURES * 8 + r, FEATURES, stride=8), :] for p in range(per_tile)], axis=1
                )

            write(0, jnp.concatenate(list(distance) + [zero[0:3]], axis=0))
            for i in range(FEATURES):
                value = zero
                if i < 4:
                    value = far * dipole[i] + lifted * distance[i]
                elif i == 4:
                    value = lifted * distance[i]
                keep(i, value)
            for m in range(3):
                for part in range(2):
                    write(1 + 4 * m + part, gathered(2 * m + part))
            for i in range(FEATURES):
                keep(i, near * dipole[i] if i < 4 else zero)
            for m in range(3):
                for part in range(2):
                    write(3 + 4 * m + part, gathered(2 * m + part))
            return carry

        lax.fori_loop(0, held, one, 0)

    def pair_sums(chosen):
        def step(it, carry):
            at = pl.multiple_of(it // held * CHUNK, CHUNK)
            j = it % held
            feat = feat_ref[pl.ds(at, CHUNK), :]

            def pair(o):
                return jnp.dot(feat, coef_ref[o, j], preferred_element_type=jnp.float32)

            squares = pair(0)
            pairs = {m: [pair(4 * m - 3 + i) for i in range(4)] for m in chosen}
            for v in range(CHUNK // 8):
                obs_rows = pl.ds(pl.multiple_of(at + v * 8, 8), 8)
                t0 = hub_ref[obs_rows, :]
                sums = {}
                for lane in range(TILE // LANES):
                    where = (slice(v * 8, v * 8 + 8), slice(lane * LANES, (lane + 1) * LANES))
                    t, factors = pair_factors(squares[where], t0, chosen)
                    for m in chosen:
                        cosine, sine = factors[m]
                        p_re, p_im, m_re, m_im = (matrix[where] for matrix in pairs[m])
                        real = p_re - t * m_im
                        imag = p_im + t * m_re
                        new = (cosine * real + sine * imag, cosine * imag - sine * real)
                        old = sums.get(m)
                        sums[m] = new if old is None else (old[0] + new[0], old[1] + new[1])
                for m in chosen:
                    for part in range(2):
                        o = 2 * (m - 1) + part
                        acc_ref[o, obs_rows, :] = acc_ref[o, obs_rows, :] + sums[m][part]
            return carry

        lax.fori_loop(0, observers // CHUNK * held, step, 0)

    acc_ref[...] = jnp.zeros_like(acc_ref)

    def chunk(i, carry):
        coefficients(i * held)
        pair_sums(orders)
        return carry

    lax.fori_loop(0, tiles // held, chunk, 0)

    turn = hub - jnp.round(hub)
    base = (jnp.cos(TWO_PI * turn), jnp.sin(TWO_PI * turn))
    lane_of = lax.broadcasted_iota(jnp.int32, (LANES, LANES), 1)
    collected = []
    for b in range(block_rows):
        matrix = jnp.zeros((LANES, LANES), jnp.float32)
        for o in range(2 * count):
            total = jnp.sum(acc_ref[o, b * LANES : (b + 1) * LANES, :], axis=1, keepdims=True)
            matrix = jnp.where(lane_of == o, total, matrix)
        collected.append(matrix.T[0:8])
    results = []
    phase = (jnp.ones_like(turn), jnp.zeros_like(turn))
    for m in range(count):
        phase = (phase[0] * base[0] - phase[1] * base[1], phase[0] * base[1] + phase[1] * base[0])
        real = jnp.concatenate([rows[2 * m : 2 * m + 1] for rows in collected], axis=0)
        imag = jnp.concatenate([rows[2 * m + 1 : 2 * m + 2] for rows in collected], axis=0)
        results.append((real * phase[0] + imag * phase[1], imag * phase[0] - real * phase[1]))
    for h in range(out_ref.shape[1]):
        for part in range(2):
            value = results[-1][part]
            for m in range(count - 1, 0, -1):
                value = jnp.where(harm_ref[h] == m, results[m - 1][part], value)
            out_ref[part, h] = value


def transform_table(instances, comps):
    orders = np.arange(1, 4)
    angles = 2.0 * np.pi * (orders[:, None] * np.arange(instances)[None, :] % instances) / instances
    real, imag = np.cos(angles) / instances, -np.sin(angles) / instances
    table = np.zeros((comps * 8, instances * comps), np.float64)
    for c in range(comps):
        for m in range(3):
            pair = (-imag[m], real[m]) if c == 0 else (real[m], imag[m])
            for part in range(2):
                table[c * 8 + 2 * m + part, c::comps] = pair[part]
    bf16 = jnp.bfloat16
    high = table.astype(bf16)
    middle = (table - high.astype(np.float64)).astype(bf16)
    low = (table - high.astype(np.float64) - middle.astype(np.float64)).astype(bf16)
    return np.stack([high, middle, low])


def per_device(
    sources, panel_positions, panel_copy, harmonic_numbers, blade_count, observer_ids, observer_radius, *, sizes,
):
    axes = ("inst", "panel", "obs")
    insts = sizes["inst"]
    devices = math.prod(sizes[axis] for axis in axes)
    per_inst, comps, own_panels = sources.shape
    rows = per_inst * comps + 8
    block_rows = observer_ids.shape[1] // (insts * sizes["panel"])
    observers = block_rows * LANES
    tiles = devices // insts * own_panels // TILE
    held = min(HELD_TILES, tiles)
    smem = pl.BlockSpec(memory_space=pltpu.SMEM)
    vmem = pl.BlockSpec(memory_space=pltpu.VMEM)

    block = pl.pallas_call(
        pack_kernel,
        out_shape=jax.ShapeDtypeStruct((devices, rows, own_panels), jnp.bfloat16),
        in_specs=[smem, vmem, vmem, vmem],
        out_specs=vmem,
        name="pack",
    )(blade_count, sources, panel_positions, panel_copy.reshape(1, own_panels))
    got = lax.all_to_all(block, axes, split_axis=0, concat_axis=0, tiled=True)
    table = jnp.asarray(transform_table(per_inst * insts, comps))
    kernel = functools.partial(main_kernel, insts=insts, per_inst=per_inst, comps=comps, orders=(1, 2, 3))
    harmonics = harmonic_numbers.shape[0]
    pressure = pl.pallas_call(
        kernel,
        out_shape=jax.ShapeDtypeStruct((2, harmonics, block_rows, LANES), jnp.float32),
        in_specs=[smem, smem, vmem, vmem, vmem, vmem],
        out_specs=vmem,
        scratch_shapes=[
            pltpu.VMEM((observers, DEPTH), jnp.bfloat16),
            pltpu.VMEM((observers, LANES), jnp.float32),
            pltpu.VMEM((13, held, DEPTH, TILE), jnp.bfloat16),
            pltpu.VMEM((6, observers, LANES), jnp.float32),
            pltpu.VMEM((TILE // LANES * FEATURES * 8, LANES), jnp.float32),
        ],
        name="panel_sum",
    )(harmonic_numbers, blade_count, table, got, observer_ids, observer_radius)
    return jnp.transpose(pressure, (2, 0, 1, 3))[None]


def solution(mesh):
    placed = (
        P("inst", None, ("panel", "obs")),
        P(None, ("panel", "obs")),
        P(("panel", "obs")),
        P(),
        P(),
        P("obs", None, None),
        P("obs", None, None),
    )
    return jax.shard_map(
        functools.partial(per_device, sizes=dict(mesh.shape)),
        mesh=mesh,
        in_specs=placed,
        out_specs=P("obs", ("inst", "panel"), None, None, None),
        check_vma=False,
    )
```

time: 348 us -> 50.5 us (0.15)
  other arithmetic: 178 us -> 0 us
  waiting for transfers between devices: 123 us -> 0 us
  Pallas kernels: 0 us -> 31.7 us
  local copies, waits for them, and re-layouts: 21.1 us -> 1.36 us
  between operations: 16.2 us -> 0.65 us
  blocking collectives: 2.44 us -> 16.5 us
    reduce_sum x24 -> x0, other arithmetic: 171 us -> none  [one_block(): jnp.sum(addend, axis=1)]
    reduce_scatter x1 -> x0, waiting for transfers between devices: 123 us -> none  [per_device(): lax.psum_scatter(stack_rows(shaped, harmonics), ('inst', 'panel'), scatte...]
    pallas_call x0 -> x2, Pallas kernels: none -> 31.7 us  [the longest x1 30.1 us: per_device(): pl.pallas_call(kernel, out_shape=jax.ShapeDtypeStruct((2, harmonics, bloc...]
    all_to_all x0 -> x1, blocking collectives: none -> 16.5 us  [per_device(): got = lax.all_to_all(block, axes, split_axis=0, concat_axis=0, tiled=True)]
    dynamic_update_slice x48 -> x0, local copies, waits for them, and re-layouts: 9.75 us -> none  [one_tile(): return (lax.map(one_block, (block_coords, current)), None)]
    slice x12 -> x0, local copies, waits for them, and re-layouts: 5.87 us -> none  [the longest x9 5.85 us: panel_term(): wavenumber = wavenumbers[number]]
    mul x3 -> x0, other arithmetic: 5.78 us -> none  [the longest x1 3.72 us: observer_coords(): observer_radius * sine_theta * jnp.sin(azimuth)]
  transfers between devices with their start and end apart: 2 -> 0, of which waited for: 1 -> 0; matrix products, arithmetic and copies ran while one was open for 2% -> 0% of each run, Pallas kernels for 0% -> 0%
where the time goes in v1:
time: 50.5 us; the launch traced here: 50.2 us
  Pallas kernels  31.7 us (63%)
  blocking collectives  16.5 us (33%)
  local copies, waits for them, and re-layouts  1.36 us (3%)
  between operations  0.65 us (1%)
    pallas_call x1, Pallas kernels, per_device(): pl.pallas_call(kernel, out_shape=jax.ShapeDtypeStruct((2, harmonics, bloc...  30.1 us
    all_to_all x1, blocking collectives, per_device(): got = lax.all_to_all(block, axes, split_axis=0, concat_axis=0, tiled=True)  16.5 us
    pallas_call x1, Pallas kernels, per_device(): pl.pallas_call(pack_kernel, out_shape=jax.ShapeDtypeStruct((devices, rows...  1.63 us
    broadcast_in_dim x1, local copies, waits for them, and re-layouts, per_device(): return jnp.transpose(pressure, (2, 0, 1, 3))[None]  1.36 us

profile of v1, /device:TPU:1, one launch (start us, length us, event | category | flops | bytes accessed | tf_op | source)
XLA Modules:
  0.0 50.2 jit_solution(15058409340813836810)
XLA Ops:
  0.7 1.6 %pack.1 = bf16[32,24,128]{2,1,0:T(8,128)(2,1)} custom-call(s32[1]{0:T(128)S(6)} %copy.10.blades_ref, bf16[4,4,128]{2,1,0:T(4,128)(2,1)} %src_ref.1, f32[3,128]{1,0:T(4,128)} %pos_ref.1, s32[1,128]{1,0:T(1,128)} %bitcast.5), custom_call_target="tpu_custom_call" | custom-call | tf_op jit(solution)/shard_map/pack/pallas_call | solution.py:292
  2.3 16.5 %all_to_all.5.got_ref = bf16[32,24,128]{2,1,0:T(8,128)(2,1)} all-to-all(bf16[32,24,128]{2,1,0:T(8,128)(2,1)} %pack.1), channel_id=1, replica_groups=mesh['inst'=2,'panel'=8,'obs'=2] {'inst','panel','obs'}, dimensions={0} | all-to-all | bytes 393216 | tf_op jit(solution)/shard_map/all_to_all | solution.py:299
  18.7 30.1 %panel_sum.1 = f32[2,3,8,128]{3,2,1,0:T(8,128)} custom-call(s32[3]{0:T(128)} %harm_ref.1, s32[1]{0:T(128)S(6)} %copy.10.blades_ref, bf16[3,32,32]{2,1,0:T(8,128)(2,1)} %constant.2.clone.table_ref, bf16[32,24,128]{2,1,0:T(8,128)(2,1)} %all_to_all.5.got_ref, s32[1,128,128]{2,1,0:T(8,128)} %ids_ref.1, f32[1,128,128]{2,1,0:T(8,128)} %radius_ref.1), custom_call_target="tpu_custom_call" | custom-call | tf_op jit(solution)/shard_map/panel_sum/pallas_call | solution.py:303
  48.8 1.4 %copy.9 = f32[1,8,2,3,128]{4,2,3,1,0:T(2,128)} copy(f32[1,8,2,3,128]{4,1,3,2,0:T(8,128)} %bitcast.4) | data formatting | bytes 49152 | tf_op jit(solution)/shard_map/broadcast_in_dim | solution.py:317

commit v2 on v1

--- a/solution.py
+++ b/solution.py
@@ -15,7 +15,7 @@
 TWO_PI = 2.0 * 3.141592653589793
 LANES = 128
 TILE = 256
-CHUNK = 256
+CHUNK = 512
 HELD_TILES = 8
 FEATURES = 8
 PARTS = 6
@@ -65,13 +65,15 @@
     twice = 2.0 - q
     d = 4.0 - q
     cosine = w3 * twice
-    sine = w3 * (s * (d * lax.rsqrt(d)))
+    sine = w3 * (s * (1.0 / lax.rsqrt(d)))
     factors = {1: (cosine, sine)}
-    if orders[-1] > 1:
+    if 2 in orders:
         factors[2] = (twice * cosine - (w3 + w3), twice * sine)
-    for m in range(3, orders[-1] + 1):
-        (c1, s1), (c0, s0) = factors[m - 1], factors[m - 2]
-        factors[m] = (twice * c1 - c0, twice * s1 - s0)
+        if 3 in orders:
+            factors[3] = (twice * factors[2][0] - cosine, twice * factors[2][1] - sine)
+    elif 3 in orders:
+        square = twice * twice
+        factors[3] = (cosine * (square - 3.0), sine * (square - 1.0))
     return t, factors
 
 
@@ -79,7 +81,7 @@
     harm_ref, blades_ref, table_ref, got_ref, ids_ref, radius_ref, out_ref,
     feat_ref, hub_ref, coef_ref, acc_ref, rows_ref, *, insts, per_inst, comps, orders,
 ):
-    block_rows = out_ref.shape[2]
+    block_rows = out_ref.shape[0]
     observers = block_rows * LANES
     groups = got_ref.shape[0] // insts
     tiles = groups * LANES // TILE
@@ -225,9 +227,17 @@
 
     acc_ref[...] = jnp.zeros_like(acc_ref)
 
+    asked = [functools.reduce(jnp.logical_or, [harm_ref[h] == m for h in range(out_ref.shape[1])]) for m in orders]
+    which = sum(jnp.where(present, 1 << i, 0) for i, present in enumerate(asked))
+
     def chunk(i, carry):
         coefficients(i * held)
-        pair_sums(orders)
+        for bits in range(1, 1 << count):
+
+            @pl.when(which == bits)
+            def _():
+                pair_sums(tuple(m for k, m in enumerate(orders) if bits >> k & 1))
+
         return carry
 
     lax.fori_loop(0, tiles // held, chunk, 0)
@@ -254,7 +264,7 @@
             value = results[-1][part]
             for m in range(count - 1, 0, -1):
                 value = jnp.where(harm_ref[h] == m, results[m - 1][part], value)
-            out_ref[part, h] = value
+            out_ref[:, h, part, :] = value
 
 
 def transform_table(instances, comps):
@@ -302,7 +312,7 @@
     harmonics = harmonic_numbers.shape[0]
     pressure = pl.pallas_call(
         kernel,
-        out_shape=jax.ShapeDtypeStruct((2, harmonics, block_rows, LANES), jnp.float32),
+        out_shape=jax.ShapeDtypeStruct((block_rows, harmonics, 2, LANES), jnp.float32),
         in_specs=[smem, smem, vmem, vmem, vmem, vmem],
         out_specs=vmem,
         scratch_shapes=[
@@ -314,7 +324,7 @@
         ],
         name="panel_sum",
     )(harmonic_numbers, blade_count, table, got, observer_ids, observer_radius)
-    return jnp.transpose(pressure, (2, 0, 1, 3))[None]
+    return jnp.transpose(pressure, (0, 2, 1, 3))[None]
 
 
 def solution(mesh):

time: 50.5 us -> 43.8 us (0.87)
  Pallas kernels: 31.7 us -> 26.5 us
  local copies, waits for them, and re-layouts: 1.36 us -> 0 us
    pallas_call x1, Pallas kernels: 30.1 us -> 24.9 us  [per_device(): pl.pallas_call(kernel, out_shape=jax.ShapeDtypeStruct((block_rows, harmon...]
    broadcast_in_dim x1 -> x0, local copies, waits for them, and re-layouts: 1.36 us -> none  [per_device(): return jnp.transpose(pressure, (2, 0, 1, 3))[None]]
where the time goes in v2:
time: 43.8 us; the launch traced here: 43.6 us
  Pallas kernels  26.5 us (61%)
  blocking collectives  16.5 us (38%)
  between operations  0.65 us (1%)
    pallas_call x1, Pallas kernels, per_device(): pl.pallas_call(kernel, out_shape=jax.ShapeDtypeStruct((block_rows, harmon...  24.9 us
    all_to_all x1, blocking collectives, per_device(): got = lax.all_to_all(block, axes, split_axis=0, concat_axis=0, tiled=True)  16.5 us
    pallas_call x1, Pallas kernels, per_device(): pl.pallas_call(pack_kernel, out_shape=jax.ShapeDtypeStruct((devices, rows...  1.62 us

profile of v2, /device:TPU:1, one launch (start us, length us, event | category | flops | bytes accessed | tf_op | source)
XLA Modules:
  0.0 43.6 jit_solution(17915978821373796237)
XLA Ops:
  0.7 1.6 %pack.1 = bf16[32,24,128]{2,1,0:T(8,128)(2,1)} custom-call(s32[1]{0:T(128)S(6)} %copy.9.blades_ref, bf16[4,4,128]{2,1,0:T(4,128)(2,1)} %src_ref.1, f32[3,128]{1,0:T(4,128)} %pos_ref.1, s32[1,128]{1,0:T(1,128)} %bitcast.4), custom_call_target="tpu_custom_call" | custom-call | tf_op jit(solution)/shard_map/pack/pallas_call | solution.py:302
  2.3 16.5 %all_to_all.5.got_ref = bf16[32,24,128]{2,1,0:T(8,128)(2,1)} all-to-all(bf16[32,24,128]{2,1,0:T(8,128)(2,1)} %pack.1), channel_id=1, replica_groups=mesh['inst'=2,'panel'=8,'obs'=2] {'inst','panel','obs'}, dimensions={0} | all-to-all | bytes 393216 | tf_op jit(solution)/shard_map/all_to_all | solution.py:309
  18.7 24.9 %panel_sum.1 = f32[8,3,2,128]{3,2,1,0:T(2,128)} custom-call(s32[3]{0:T(128)} %harm_ref.1, s32[1]{0:T(128)S(6)} %copy.9.blades_ref, bf16[3,32,32]{2,1,0:T(8,128)(2,1)} %constant.2.clone.table_ref, bf16[32,24,128]{2,1,0:T(8,128)(2,1)} %all_to_all.5.got_ref, s32[1,128,128]{2,1,0:T(8,128)} %ids_ref.1, f32[1,128,128]{2,1,0:T(8,128)} %radius_ref.1), custom_call_target="tpu_custom_call" | custom-call | tf_op jit(solution)/shard_map/panel_sum/pallas_call | solution.py:313
